TPU v7x, 512 devices: a whole 4x8x8 slice. The times are simulated.
512 devices in a mesh: cells: 128 (over z, y_lo, x, core), stations: 4 (over y_hi).
Axes of the slice: x: 4, y: 8 (y_hi: 4, y_lo: 2; y = y_hi * 2 + y_lo), z: 8, core: 2. Of those that a mesh axis runs over, the one named last changes fastest.
Arguments:
- probes: bfloat16 [16, 524288], P(None, 'cells'), may hold values from -6 to 6
- reg_weight: float32 [524288], P('cells'), may hold values from 0.1 to 1
- cell_plan: int32 [2, 524288], P(None, 'cells'), may hold values from 0 to 255
- cell_depth: int32 [524288], P('cells'), may hold values from 0 to 15, as said below
- station_index: int32 [2, 16384], P(None, 'stations'), may hold values from 0 to 65535, as said below
- station_weight: float32 [16384], P('stations'), may hold values from 0.5 to 2
Outputs:
- basis: float32 [16, 524288], P(None, ('cells', 'stations'))
- factor: float32 [16, 16], replicated
Inputs may be any that keep to these rules, and one draw needn't show every extreme that they name: `cell_plan`: east and north cell indices of a grid of 256 by 256 columns. `cell_depth`: depth indices of 16 layers. `station_index`: east and north station positions in 1/256ths of a cell width, over the same area as the cells' grid.
All inputs are finite; a program needn't handle non-finite values.
Results may differ from a plain program's by a relative error of at most 0.00065.
Values may be sent and summed in bfloat16 or wider, within the bound.
No kernel may reach another device: no remote copies, remote signals or barrier semaphores. Data moves between devices by JAX's collectives and lax.ppermute only.
A program may use at most 64 MiB of HBM per device.

v0:
```python
import math
import jax
import jax.numpy as jnp
from jax import lax
from jax.sharding import PartitionSpec as P

GRAVITY = 2.0
JITTER = 1e-06
SUBSTEP = 0.00390625


def cell_points(cell_plan, cell_depth):
    cell_east = cell_plan[0].astype(jnp.float32) + 0.5
    cell_north = cell_plan[1].astype(jnp.float32) + 0.5
    cell_down = cell_depth.astype(jnp.float32) + 1.0
    return (cell_east, cell_north, cell_down)


def sensitivity(st_east, st_north, cell_geom):
    cell_east, cell_north, cell_down = cell_geom
    d_east = cell_east[None, :] - st_east[:, None]
    d_north = cell_north[None, :] - st_north[:, None]
    distance = d_east * d_east + d_north * d_north + cell_down[None, :] * cell_down[None, :]
    inverse = lax.rsqrt(distance)
    return (GRAVITY * cell_down[None, :] * inverse * inverse * inverse).astype(jnp.bfloat16)


def forward_terms(probes, st_east, st_north, cell_geom):
    station_count = st_east.shape[0]
    block_size = math.gcd(station_count, 512)

    def forward_advance(turn_index, running):
        start_at = turn_index * block_size
        sens_tile = sensitivity(
            lax.dynamic_slice_in_dim(st_east, start_at, block_size),
            lax.dynamic_slice_in_dim(st_north, start_at, block_size),
            cell_geom,
        )
        partial_value = lax.dot_general(
            probes, sens_tile, (((1,), (1,)), ((), ())), preferred_element_type=jnp.float32
        )
        return lax.dynamic_update_slice_in_dim(running, partial_value, start_at, 1)

    zero_field = jnp.zeros((probes.shape[0], station_count), jnp.float32)
    return lax.fori_loop(0, station_count // block_size, forward_advance, zero_field)


def transposed_add(running, weighted, st_east, st_north, cell_geom):
    station_count = weighted.shape[1]
    block_size = math.gcd(station_count, 512)

    def transposed_advance(turn_index, current):
        start_at = turn_index * block_size
        sens_tile = sensitivity(
            lax.dynamic_slice_in_dim(st_east, start_at, block_size),
            lax.dynamic_slice_in_dim(st_north, start_at, block_size),
            cell_geom,
        )
        segment = lax.dynamic_slice_in_dim(weighted, start_at, block_size, 1)
        return current + jnp.dot(segment, sens_tile, preferred_element_type=jnp.float32)

    return lax.fori_loop(0, station_count // block_size, transposed_advance, running)


def gram_term(hess_image):
    return jnp.dot(
        hess_image,
        hess_image.T,
        precision=lax.Precision.HIGHEST,
        preferred_element_type=jnp.float32,
    )


def body(probes, reg_weight, cell_plan, cell_depth, station_index, station_weight):
    cell_geom = cell_points(cell_plan, cell_depth)
    st_east = station_index[0].astype(jnp.float32) * SUBSTEP
    st_north = station_index[1].astype(jnp.float32) * SUBSTEP
    station_scale = station_weight * station_weight
    terms = forward_terms(probes, st_east, st_north, cell_geom)
    zero_image = jnp.zeros((probes.shape[0], probes.shape[1]), jnp.float32)
    station_field = lax.psum(terms, "cells")
    weighted = (station_scale[None, :] * station_field).astype(jnp.bfloat16)
    backward = transposed_add(zero_image, weighted, st_east, st_north, cell_geom)
    group_count = lax.axis_size("stations")
    quarter = probes.shape[1] // group_count
    offset_cells = lax.axis_index("stations") * quarter
    cell_total = probes.shape[1] * lax.axis_size("cells")
    summed = lax.psum(backward, "stations")
    hess_image = summed + reg_weight[None, :] * probes.astype(jnp.float32)
    gram_matrix = lax.psum(gram_term(hess_image), "cells")
    local_image = lax.dynamic_slice_in_dim(hess_image, offset_cells, quarter, 1)
    gram_matrix = gram_matrix / cell_total + JITTER * jnp.eye(probes.shape[0], dtype=jnp.float32)
    lower_factor = jnp.linalg.cholesky(gram_matrix)
    basis_rows = jax.scipy.linalg.solve_triangular(lower_factor, local_image, lower=True)
    return (basis_rows, lower_factor)


def solution(mesh):
    return jax.shard_map(
        body,
        mesh=mesh,
        in_specs=(
            P(None, "cells"),
            P("cells"),
            P(None, "cells"),
            P("cells"),
            P(None, "stations"),
            P("stations"),
        ),
        out_specs=(P(None, ("cells", "stations")), P()),
        check_vma=False,
    )
```

profile of v0, /device:TPU:16, one launch (start us, length us, event | category | flops | bytes accessed | tf_op | source)
XLA Modules:
  0.0 1378.7 jit_solution(104188721798137522)
XLA Ops:
  7.2 0.9 convert_add_fusion
  8.1 0.9 convert_multiply_fusion
  9.0 0.7 fusion.23
  9.7 25.5 %while.29 = (s32[]{:T(128)}, f32[16,4096]{1,0:T(8,128)S(1)}, f32[4096]{0:T(1024)S(1)}, f32[4096]{0:T(1024)S(1)}, f32[4096]{0:T(1024)S(1)}, /*index=5*/f32[4096]{...) while((s32[]{:T(128)}, f32[16,4096]{1,0:T(8,128)S(1)}, ...), condition=%wide.region_1.0_spmd, body=%wide.region_0.0_spmd.sunk | while | flops 88084488 | bytes 274615 | solution.py:45
  9.7 0.1 dynamic_slice.56
  9.9 3.0 fusion.35
  12.9 0.1 dynamic_slice.56
  13.1 3.0 fusion.35
  16.3 3.0 fusion.35
  19.4 0.1 dynamic_slice.57
  19.5 3.0 fusion.35
  22.5 0.1 dynamic_slice.56
  22.6 0.1 dynamic_slice.57
  22.6 3.0 fusion.35
  25.7 0.1 dynamic_slice.56
  25.8 3.0 fusion.35
  29.0 3.0 fusion.35
  32.2 3.0 fusion.35
  35.2 0.7 copy-done
  36.1 966.5 %all-reduce.3.cloned.1.call-done = f32[16,4096]{1,0:T(8,128)} async-done(((f32[16,4096]{1,0:T(8,128)}), f32[16,4096]{1,0:T(8,128)}) %all-reduce.3.cloned.1.call-update) | async-done | bytes 262160 | tf_op jit(solution)/shard_map/psum | solution.py:81
  1002.5 1.0 multiply_convert_fusion
  1003.5 25.6 %while.30 = (s32[]{:T(128)}, f32[16,4096]{1,0:T(8,128)S(1)}, bf16[16,4096]{1,0:T(8,128)(2,1)S(1)}, f32[4096]{0:T(1024)S(1)}, f32[4096]{0:T(1024)S(1)}, /*index=5...) while((s32[]{:T(128)}, f32[16,4096]{1,0:T(8,128)S(1)}, ...), condition=%wide.region_4.0_spmd.clone, body=%wide.region_3.0_spmd.clone.sunk | while | flops 88215560 | bytes 651457 | solution.py:62
  1003.5 0.1 dynamic_slice.59
  1003.7 3.0 convolution_add_fusion.2
  1006.7 0.1 dynamic_slice.59
  1006.9 3.0 convolution_add_fusion.2
  1009.9 0.1 dynamic_slice.59
  1010.1 3.0 convolution_add_fusion.2
  1013.1 0.1 dynamic_slice.59
  1013.3 3.0 convolution_add_fusion.2
  1016.3 0.1 dynamic_slice.59
  1016.5 3.0 convolution_add_fusion.2
  1019.5 0.1 dynamic_slice.59
  1019.7 3.0 convolution_add_fusion.2
  1022.7 0.1 dynamic_slice.59
  1022.9 3.0 convolution_add_fusion.2
  1025.9 0.1 dynamic_slice.59
  1026.1 3.0 convolution_add_fusion.2
  1029.2 0.7 copy-done.1
  1029.9 51.8 %all-reduce.5.cloned.1.call-done = f32[16,4096]{1,0:T(8,128)} async-done(((f32[16,4096]{1,0:T(8,128)}), f32[16,4096]{1,0:T(8,128)}) %all-reduce.5.cloned.1.call-update) | async-done | bytes 262160 | tf_op jit(solution)/shard_map/psum | solution.py:88
  1081.7 1.0 multiply_add_fusion
  1082.7 0.5 fusion.24
  1083.1 283.1 %psum.23 = f32[16,16]{1,0:T(8,128)S(1)} all-reduce(f32[16,16]{1,0:T(8,128)S(1)} %fusion.24), channel_id=1, replica_groups=mesh['cells'=128,'stations'=4] {'cells'}, use_global_device_ids=true, to_apply=%region_6.0 | all-reduce | flops 256 | bytes 2048 | tf_op jit(solution)/shard_map/psum | solution.py:90
  1366.3 1.5 cholesky.16
  1367.8 0.6 compare_reduce_fusion
  1368.5 1.2 select_bitcast_fusion
  1369.7 1.2 custom-call.7
  1370.9 0.9 fusion.18
  (53 shorter events, 1.7 us)
Async XLA Ops:
  7.2 2.6 copy-start.2
  7.2 995.4 %all-reduce.3.cloned.1.call-start = ((), (), s32[]{:S(2)}) async-start(), calls=%async_computation | async-start | bytes 524288 | tf_op jit(solution)/shard_map/psum | solution.py:81
  35.2 0.7 copy-start
  35.2 0.8 copy-start.3
  36.0 1045.7 %all-reduce.5.cloned.1.call-start = ((), (), s32[]{:S(2)}) async-start(), calls=%async_computation.1 | async-start | bytes 524288 | tf_op jit(solution)/shard_map/psum | solution.py:88
  1029.1 0.7 copy-start.1
  1029.1 52.5 %copy-start.4 = (f32[4096]{0:T(1024)S(1)}, f32[4096]{0:T(1024)}, u32[]{:S(2)}) copy-start(f32[4096]{0:T(1024)} %param.11) | copy-start | bytes 49156
Sparse Core Ops, SparseCore 0:
  36.1 966.3 all-reduce.2
  1030.0 51.6 all-reduce.4
where the time goes:
time: 1380 us
  waiting for transfers between devices  1020 us (74%)
  blocking collectives  283 us (21%)
  matrix products  50 us (4%)
  between operations  14.1 us (1%)
    psum x1, waiting for transfers between devices, body(): station_field = lax.psum(terms, 'cells')  966 us
    psum x1, blocking collectives, body(): gram_matrix = lax.psum(gram_term(hess_image), 'cells')  283 us
    psum x1, waiting for transfers between devices, body(): summed = lax.psum(backward, 'stations')  51.8 us
  transfers between devices with their start and end apart: 2, of which 2 were waited for; matrix products, arithmetic and copies ran while one was open for 0% of the time, Pallas kernels for 0%

commit v1 on v0

--- a/solution.py
+++ b/solution.py
@@ -78,7 +78,7 @@
     station_scale = station_weight * station_weight
     terms = forward_terms(probes, st_east, st_north, cell_geom)
     zero_image = jnp.zeros((probes.shape[0], probes.shape[1]), jnp.float32)
-    station_field = lax.psum(terms, "cells")
+    station_field = jnp.sum(lax.all_gather(terms, "cells"), axis=0)
     weighted = (station_scale[None, :] * station_field).astype(jnp.bfloat16)
     backward = transposed_add(zero_image, weighted, st_east, st_north, cell_geom)
     group_count = lax.axis_size("stations")

time: 1380 us -> 692 us (0.50)
  waiting for transfers between devices: 1020 us -> 313 us
    psum x1 -> x0, waiting for transfers between devices: 966 us -> none  [body(): station_field = lax.psum(terms, 'cells')]
    all_gather x0 -> x1, waiting for transfers between devices: none -> 259 us  [body(): station_field = jnp.sum(lax.all_gather(terms, 'cells'), axis=0)]
where the time goes in v1:
time: 692 us; the launch traced here: 691 us
  waiting for transfers between devices  313 us (45%)
  blocking collectives  283 us (41%)
  matrix products  57.2 us (8%)
  other arithmetic  20 us (3%)
  between operations  14.1 us (2%)
    psum x1, blocking collectives, body(): gram_matrix = lax.psum(gram_term(hess_image), 'cells')  283 us
    all_gather x1, waiting for transfers between devices, body(): station_field = jnp.sum(lax.all_gather(terms, 'cells'), axis=0)  259 us
    psum x1, waiting for transfers between devices, body(): summed = lax.psum(backward, 'stations')  53.2 us
    dot_general x8, matrix products, forward_advance(): lax.dot_general(probes, sens_tile, (((1,), (1,)), ((), ())), preferred_el...  31.5 us
    dot_general x8, matrix products, transposed_advance(): jnp.dot(segment, sens_tile, preferred_element_type=jnp.float32)  24.4 us
  transfers between devices with their start and end apart: 2, of which 2 were waited for; matrix products, arithmetic and copies ran while one was open for 0% of the time, Pallas kernels for 0%

profile of v1, /device:TPU:16, one launch (start us, length us, event | category | flops | bytes accessed | tf_op | source)
XLA Modules:
  0.0 691.3 jit_solution(2072303943453521960)
XLA Ops:
  7.2 0.9 convert_add_fusion
  8.1 0.9 convert_multiply_fusion
  9.0 0.7 fusion.23
  9.7 32.7 %while.29 = (s32[]{:T(128)}, f32[16,4096]{1,0:T(8,128)S(1)}, f32[4096]{0:T(1024)S(1)}, f32[4096]{0:T(1024)S(1)}, f32[4096]{0:T(1024)S(1)}, /*index=5*/f32[4096]{...) while((s32[]{:T(128)}, f32[16,4096]{1,0:T(8,128)S(1)}, ...), condition=%wide.region_1.0_spmd, body=%wide.region_0.0_spmd.sunk | while | flops 88084488 | bytes 274615 | solution.py:45
  9.7 0.1 dynamic_slice.56
  9.9 3.9 fusion.35
  14.0 3.9 fusion.35
  18.0 0.1 dynamic_slice.57
  18.1 3.9 fusion.35
  22.0 0.1 dynamic_slice.56
  22.1 0.1 dynamic_slice.57
  22.2 3.9 fusion.35
  26.2 3.9 fusion.35
  30.2 0.1 dynamic_slice.56
  30.3 0.1 dynamic_slice.57
  30.3 3.9 fusion.35
  34.4 3.9 fusion.35
  38.5 3.9 fusion.35
  42.5 0.7 copy-done
  43.3 259.5 %all-gather.3.cloned.1.call-done = f32[2048,4096]{1,0:T(8,128)} async-done(((f32[16,4096]{1,0:T(8,128)}), f32[2048,4096]{1,0:T(8,128)}) %all-gather.3.cloned.1.call-update) | async-done | bytes 33554448 | tf_op jit(solution)/shard_map/all_gather | solution.py:81
  302.8 11.9 %reduce_sum.9 = f32[16,4096]{1,0:T(8,128)S(1)} reduce(f32[128,16,4096]{2,1,0:T(8,128)} %bitcast.32, f32[]{:T(128)} %constant.137.clone.1), dimensions={0}, to_apply=%region_2.0 | reduce | flops 8323072 | bytes 33816580 | tf_op jit(solution)/shard_map/reduce_sum | solution.py:81
  314.7 25.6 %while.30 = (s32[]{:T(128)}, f32[16,4096]{1,0:T(8,128)S(1)}, bf16[16,4096]{1,0:T(8,128)(2,1)S(1)}, f32[4096]{0:T(1024)S(1)}, f32[4096]{0:T(1024)S(1)}, /*index=5...) while((s32[]{:T(128)}, f32[16,4096]{1,0:T(8,128)S(1)}, ...), condition=%wide.region_4.0_spmd.clone, body=%wide.region_3.0_spmd.clone.sunk | while | flops 88215560 | bytes 651457 | solution.py:62
  314.7 0.1 dynamic_slice.59
  314.9 3.0 convolution_add_fusion.2
  317.9 0.1 dynamic_slice.59
  318.1 3.0 convolution_add_fusion.2
  321.1 0.1 dynamic_slice.59
  321.3 3.0 convolution_add_fusion.2
  324.3 0.1 dynamic_slice.59
  324.5 3.0 convolution_add_fusion.2
  327.5 0.1 dynamic_slice.59
  327.7 3.0 convolution_add_fusion.2
  330.7 0.1 dynamic_slice.59
  330.9 3.0 convolution_add_fusion.2
  333.9 0.1 dynamic_slice.59
  334.1 3.0 convolution_add_fusion.2
  337.1 0.1 dynamic_slice.59
  337.3 3.0 convolution_add_fusion.2
  340.4 0.7 copy-done.1
  341.1 53.2 %all-reduce.2.cloned.1.call-done = f32[16,4096]{1,0:T(8,128)} async-done(((f32[16,4096]{1,0:T(8,128)}), f32[16,4096]{1,0:T(8,128)}) %all-reduce.2.cloned.1.call-update) | async-done | bytes 262160 | tf_op jit(solution)/shard_map/psum | solution.py:88
  394.3 1.0 multiply_add_fusion
  395.2 0.4 fusion.24
  395.7 283.1 %psum.15 = f32[16,16]{1,0:T(8,128)S(1)} all-reduce(f32[16,16]{1,0:T(8,128)S(1)} %fusion.24), channel_id=1, replica_groups=mesh['cells'=128,'stations'=4] {'cells'}, use_global_device_ids=true, to_apply=%region_6.0 | all-reduce | flops 256 | bytes 2048 | tf_op jit(solution)/shard_map/psum | solution.py:90
  678.9 1.5 cholesky.16
  680.4 0.6 compare_reduce_fusion
  681.0 1.2 select_bitcast_fusion
  682.3 1.2 custom-call.7
  683.5 0.9 fusion.18
  (54 shorter events, 1.7 us)
Async XLA Ops:
  7.2 295.6 %all-gather.3.cloned.1.call-start = ((), (), s32[]{:S(2)}) async-start(), calls=%async_computation.1 | async-start | bytes 33816576 | tf_op jit(solution)/shard_map/all_gather | solution.py:81
  9.7 33.6 %copy-start.3 = (f32[4096]{0:T(1024)S(1)}, f32[4096]{0:T(1024)}, u32[]{:S(2)}) copy-start(f32[4096]{0:T(1024)} %param.15) | copy-start | bytes 49156
  42.5 0.7 copy-start
  43.2 351.0 %all-reduce.2.cloned.1.call-start = ((), (), s32[]{:S(2)}) async-start(), calls=%async_computation | async-start | bytes 524288 | tf_op jit(solution)/shard_map/psum | solution.py:88
  314.7 79.6 %copy-start.2 = (bf16[16,4096]{1,0:T(8,128)(2,1)S(1)}, bf16[16,4096]{1,0:T(8,128)(2,1)}, u32[]{:S(2)}) copy-start(bf16[16,4096]{1,0:T(8,128)(2,1)} %get-tuple-element.627) | copy-start | bytes 393220
  314.7 79.6 %copy-start.4 = (f32[4096]{0:T(1024)S(1)}, f32[4096]{0:T(1024)}, u32[]{:S(2)}) copy-start(f32[4096]{0:T(1024)} %param.11) | copy-start | bytes 49156
  340.3 0.7 copy-start.1
Sparse Core Ops, SparseCore 0:
  43.3 259.4 all-gather.2
  341.2 53.0 all-reduce.1
